TPU v7x, 32 devices: a whole 2x2x4 slice. The times are simulated.
32 devices in a mesh: groups: 2 (over y), fsdp: 2 (over core), ep: 8 (over z, x).
Axes of the slice: x: 2, y: 2, z: 4, core: 2. Of those that a mesh axis runs over, the one named last changes fastest.
Arguments:
- tokens: bfloat16 [32, 7168], P(('groups', 'fsdp', 'ep')), parts along dimension 0, may hold values from -6 to 6
- gate_weight: bfloat16 [7168, 1024], P('fsdp', 'ep'), may hold values from -0.0625 to 0.0625
- up_weight: bfloat16 [7168, 1024], P('fsdp', 'ep'), may hold values from -0.0625 to 0.0625
- down_weight: bfloat16 [1024, 7168], P('ep', 'fsdp'), may hold values from -0.1875 to 0.1875
- steering: bfloat16 [1, 7168], replicated, may hold values from -3 to 3
- block_rows: int32 [2, 2, 8], P(None, 'groups'), parts along dimension 1, may hold values from 0 to 7, as said below
- block_gates: float32 [2, 2, 8], P(None, 'groups'), parts along dimension 1, may hold values from 0 to 1, as said below
Outputs:
- mixed: bfloat16 [32, 7168], P(('groups', 'fsdp', 'ep')), parts along dimension 0
There are 2 independent parts, one for each index of `groups`. A program takes and returns all parts, laid end to end along the dimension named above; an argument that names none is the same for every part. Nothing has to cross between parts.
Inputs may be any that keep to these rules, and one draw needn't show every extreme that they name: `block_rows`: within one block the 8 token numbers are distinct. `block_gates`: in each block the gates are positive and falling on the first slots and zero on the rest; in each half one block has no zero gate.
All inputs are finite; a program needn't handle non-finite values.
Results may differ from a plain program's by a relative error of at most 0.0049.
Values may be sent and summed in bfloat16 or wider, within the bound.
No kernel may reach another device: no remote copies, remote signals or barrier semaphores. Data moves between devices by JAX's collectives and lax.ppermute only.
A program may use at most 64 MiB of HBM per device.

v0:
```python
import jax
import jax.numpy as jnp
from jax import lax
from jax.sharding import PartitionSpec as P


def body(tokens, gate_weight, up_weight, down_weight, steering, block_rows, block_gates):
    tok_rows = lax.all_gather(tokens, "ep", axis=0, tiled=True)
    slice_units = gate_weight.shape[1]
    window_experts = block_rows.shape[1]
    ep_count = lax.axis_size("ep")
    window_width = ep_count * slice_units // window_experts
    group_size = window_width // slice_units
    position = lax.axis_index("ep")
    expert = position // group_size
    member = position % group_size
    half_index = lax.axis_index("fsdp")
    expert_rows = lax.dynamic_index_in_dim(block_rows, expert, 1, keepdims=False)
    expert_gates = lax.dynamic_index_in_dim(block_gates, expert, 1, keepdims=False)
    slot_rows = lax.dynamic_index_in_dim(expert_rows, half_index, 0, keepdims=False)
    slot_gates = lax.dynamic_index_in_dim(expert_gates, half_index, 0, keepdims=False)
    picked = jnp.take(tok_rows, slot_rows, axis=0)
    gate_pre = jnp.dot(
        picked,
        lax.all_gather(gate_weight, "fsdp", axis=0, tiled=True),
        preferred_element_type=jnp.float32,
    )
    up_pre = jnp.dot(
        picked,
        lax.all_gather(up_weight, "fsdp", axis=0, tiled=True),
        preferred_element_type=jnp.float32,
    )
    hidden = (jax.nn.silu(gate_pre) * up_pre).astype(jnp.bfloat16)
    half_rows = tok_rows.shape[0]
    width_all = tok_rows.shape[1]
    steer_row = lax.dynamic_index_in_dim(steering, expert, 0, keepdims=False).astype(jnp.float32)
    projected = jnp.dot(
        hidden,
        lax.all_gather(down_weight, "fsdp", axis=1, tiled=True),
        preferred_element_type=jnp.float32,
    )
    leader = (member == 0).astype(jnp.float32)
    weighted = slot_gates[:, None] * (projected + leader * steer_row[None, :])
    partial_sum = jnp.zeros((half_rows, width_all), jnp.float32).at[slot_rows].add(weighted)
    summed = lax.psum_scatter(partial_sum, "ep", scatter_dimension=0, tiled=True)
    return summed.astype(jnp.bfloat16)


def solution(mesh):
    placed = (
        P(("groups", "fsdp", "ep"), None),
        P("fsdp", "ep"),
        P("fsdp", "ep"),
        P("ep", "fsdp"),
        P(),
        P(None, "groups", None),
        P(None, "groups", None),
    )
    return jax.shard_map(
        body,
        mesh=mesh,
        in_specs=placed,
        out_specs=P(("groups", "fsdp", "ep"), None),
        check_vma=False,
    )
```

profile of v0, /device:TPU:0, one launch (start us, length us, event | category | flops | bytes accessed | tf_op | source)
XLA Modules:
  0.0 99.3 jit_solution(15042454936637568538)
XLA Ops:
  6.5 0.0 copy-start
  6.5 0.0 all-gather.5.cloned.1.call-start
  6.5 0.7 all-gather.5.cloned.1.call-update
  7.3 0.0 copy-start.4
  7.3 0.0 copy-start.1
  7.3 0.0 all-gather.7.cloned.1.call-start
  7.3 0.7 all-gather.7.cloned.1.call-update
  8.0 0.0 all-gather.9.cloned.1.call-start
  8.1 0.7 all-gather.9.cloned.1.call-update
  8.8 0.0 copy-done.3
  8.9 0.0 copy-done.2
  8.9 32.5 %all-gather = bf16[8,1,7168]{2,1,0:T(2,128)(2,1)S(1)} all-gather(bf16[1,1,7168]{2,1,0:T(2,128)(2,1)S(1)} %bitcast.19), channel_id=1, replica_groups=mesh['groups'=2,'fsdp'=2,'ep'=8] {'ep'}, dimensions={0}, use_global_device_ids=true | all-gather | bytes 129024 | tf_op jit(solution)/shard_map/all_gather | solution.py:8
  41.4 0.0 copy-done
  41.4 0.6 gather_fusion
  42.0 0.0 copy-done.4
  42.1 0.6 dynamic-slice.2
  42.7 0.0 all-gather.5.cloned.1.call-done
  42.7 2.0 %fusion.4 = f32[8,128]{1,0:T(8,128)S(1)} fusion(bf16[7168,128]{1,0:T(8,128)(2,1)} %all-gather.5.cloned.1.call-done, bf16[8,7168]{1,0:T(8,128)(2,1)S(1)} %gather_fusion, pred[8]{0:T(512)(128)(4,1)S(1)} %compare_and_fusion), kind=kOutput, calls=%fused_computation.10 | convolution fusion | flops 14737408 | bytes 1953800 | tf_op jit(solution)/shard_map/dot_general | solution.py:23
  44.7 0.0 all-gather.7.cloned.1.call-done
  44.8 2.9 %all-gather.9.cloned.1.call-done = bf16[128,7168]{1,0:T(8,128)(2,1)} async-done(((bf16[128,3584]{1,0:T(8,128)(2,1)}), bf16[128,7168]{1,0:T(8,128)(2,1)}) %all-gather.9.cloned.1.call-update) | async-done | bytes 1835024 | tf_op jit(solution)/shard_map/all_gather | solution.py:39
  47.7 2.8 %fusion = f32[8,7168]{1,0:T(8,128)S(1)} fusion(bf16[128,7168]{1,0:T(8,128)(2,1)} %all-gather.9.cloned.1.call-done, bf16[7168,128]{1,0:T(8,128)(2,1)} %all-gather.7.cloned.1.call-done, f32[7168]{0:T(1024)S(1)} %bitcast.18, f32[8]{0:T(128)S(1)} %dynamic-slice_bitcast_fusion, bf16[8,7168]{1,0:T(8,128)(2,1)S(1)} %gather_fusion, ...), kind=kOutput, calls=%fused_computation.3 | convolution fusion | flops 29538304 | bytes 4046888 | tf_op jit(solution)/shard_map/dot_general | solution.py:37
  50.5 0.9 scatter_custom_fusion
  51.4 40.1 %all-reduce.2 = bf16[8,7168]{1,0:T(8,128)(2,1)S(1)} all-reduce(f32[8,7168]{1,0:T(8,128)S(1)} %scatter_custom_fusion), channel_id=2, replica_groups=mesh['groups'=2,'fsdp'=2,'ep'=8] {'ep'}, use_global_device_ids=true, to_apply=%region_1.2.clone | all-reduce | flops 57344 | bytes 344064
  91.5 1.2 %dynamic-slice_convert_fusion = bf16[1,7168]{1,0:T(2,128)(2,1)} fusion(bf16[8,7168]{1,0:T(8,128)(2,1)S(1)} %all-reduce.2, u32[]{:T(128)} %bitcast.6), kind=kLoop, calls=%fused_computation.11 | loop fusion | bytes 28676 | tf_op jit(solution)/shard_map/convert_element_type | solution.py:46
  (9 shorter events, 0.1 us)
Async XLA Ops:
  6.5 34.9 %copy-start = (f32[2,1,8]{2,1,0:T(1,128)S(1)}, f32[2,1,8]{2,1,0:T(1,128)}, u32[]{:S(2)}) copy-start(f32[2,1,8]{2,1,0:T(1,128)} %param.13) | copy-start | bytes 196
  6.5 2.2 %copy-start.3 = (s32[2,1,8]{2,1,0:T(1,128)S(1)}, s32[2,1,8]{2,1,0:T(1,128)}, u32[]{:S(2)}) copy-start(s32[2,1,8]{2,1,0:T(1,128)} %param.12) | copy-start | bytes 196
  6.5 2.3 %copy-start.2 = (bf16[1,7168]{1,0:T(2,128)(2,1)S(1)}, bf16[1,7168]{1,0:T(2,128)(2,1)}, u32[]{:S(2)}) copy-start(bf16[1,7168]{1,0:T(2,128)(2,1)} %param.7) | copy-start | bytes 43012
  6.5 36.1 %all-gather.5.cloned.1.call-start = ((), (), s32[]{:S(2)}) async-start(), calls=%async_computation | async-start | bytes 2752512 | tf_op jit(solution)/shard_map/all_gather | solution.py:25
  7.3 34.8 %copy-start.4 = (u32[32]{0:T(128)S(1)}, u32[32]{0:T(128)}, u32[]{:S(2)}) copy-start(u32[32]{0:T(128)} %constant.79) | copy-start | bytes 388
  7.3 35.4 %copy-start.1 = (bf16[1,7168]{1,0:T(2,128)(2,1)S(1)}, bf16[1,7168]{1,0:T(2,128)(2,1)}, u32[]{:S(2)}) copy-start(bf16[1,7168]{1,0:T(2,128)(2,1)} %param.11) | copy-start | bytes 43012
  7.3 37.5 %all-gather.7.cloned.1.call-start = ((), (), s32[]{:S(2)}) async-start(), calls=%async_computation.1 | async-start | bytes 2752512 | tf_op jit(solution)/shard_map/all_gather | solution.py:30
  8.0 39.7 %all-gather.9.cloned.1.call-start = ((), (), s32[]{:S(2)}) async-start(), calls=%async_computation.2 | async-start | bytes 2752512 | tf_op jit(solution)/shard_map/all_gather | solution.py:39
Sparse Core Ops, SparseCore 0:
  8.9 12.8 all-gather.4
  23.4 11.3 all-gather.6
  36.3 11.3 all-gather.8
where the time goes:
time: 99.5 us; the launch traced here: 99.3 us
  blocking collectives  72.6 us (73%)
  between operations  13.3 us (13%)
  waiting for transfers between devices  5.06 us (5%)
  matrix products  4.84 us (5%)
  local copies, waits for them, and re-layouts  2.47 us (2%)
    unnamed x1, blocking collectives  40.1 us
    all_gather x1, blocking collectives, body(): tok_rows = lax.all_gather(tokens, 'ep', axis=0, tiled=True)  32.5 us
    all_gather x1, waiting for transfers between devices, body(): lax.all_gather(down_weight, 'fsdp', axis=1, tiled=True)  2.95 us
    dot_general x1, matrix products, body(): jnp.dot(hidden, lax.all_gather(down_weight, 'fsdp', axis=1, tiled=True),...  2.79 us
    unnamed x3, waiting for transfers between devices  2.08 us
    dot_general x1, matrix products, body(): jnp.dot(picked, lax.all_gather(gate_weight, 'fsdp', axis=0, tiled=True),...  2.05 us
  transfers between devices with their start and end apart: 3, of which 1 were waited for; matrix products, arithmetic and copies ran while one was open for 3% of the time, Pallas kernels for 0%

commit v1 on v0

--- a/solution.py
+++ b/solution.py
@@ -5,7 +5,12 @@
 
 
 def body(tokens, gate_weight, up_weight, down_weight, steering, block_rows, block_gates):
-    tok_rows = lax.all_gather(tokens, "ep", axis=0, tiled=True)
+    ring = [tokens]
+    for hop in range(7):
+        ring.append(lax.ppermute(ring[-1], "ep", [(dev, (dev + 1) % 8) for dev in range(8)]))
+    tok_rows = jnp.roll(
+        jnp.concatenate(ring[::-1], axis=0), (lax.axis_index("ep") + 1) * ring[0].shape[0], axis=0
+    )
     slice_units = gate_weight.shape[1]
     window_experts = block_rows.shape[1]
     ep_count = lax.axis_size("ep")

time: 99.5 us -> 106 us (1.065)
  waiting for transfers between devices: 5.06 us -> 45.2 us
  blocking collectives: 72.6 us -> 35.3 us
  starting transfers between devices: 0.08 us -> 3.12 us
    ppermute x0 -> x7, waiting for transfers between devices: none -> 43.7 us  [body(): lax.ppermute(ring[-1], 'ep', [(dev, (dev + 1) % 8) for dev in range(8)])]
    all_gather x1 -> x0, blocking collectives: 32.5 us -> none  [body(): tok_rows = lax.all_gather(tokens, 'ep', axis=0, tiled=True)]
    unnamed x1, blocking collectives: 40.1 us -> 35.3 us
    ppermute x0 -> x7, starting transfers between devices: none -> 3.01 us  [body(): lax.ppermute(ring[-1], 'ep', [(dev, (dev + 1) % 8) for dev in range(8)])]
    all_gather x1, waiting for transfers between devices: 2.95 us -> 0.02 us  [body(): lax.all_gather(down_weight, 'fsdp', axis=1, tiled=True)]
  transfers between devices with their start and end apart: 3 -> 10, of which waited for: 1 -> 7; matrix products, arithmetic and copies ran while one was open for 3% -> 4% of each run, Pallas kernels for 0% -> 0%
where the time goes in v1:
time: 106 us
  waiting for transfers between devices  45.2 us (43%)
  blocking collectives  35.3 us (33%)
  between operations  13.3 us (13%)
  matrix products  4.69 us (4%)
  local copies, waits for them, and re-layouts  3.34 us (3%)
  starting transfers between devices  3.12 us (3%)
    ppermute x7, waiting for transfers between devices, body(): lax.ppermute(ring[-1], 'ep', [(dev, (dev + 1) % 8) for dev in range(8)])  43.7 us
    unnamed x1, blocking collectives  35.3 us
    ppermute x7, starting transfers between devices, body(): lax.ppermute(ring[-1], 'ep', [(dev, (dev + 1) % 8) for dev in range(8)])  3.01 us
    dot_general x1, matrix products, body(): jnp.dot(hidden, lax.all_gather(down_weight, 'fsdp', axis=1, tiled=True),...  2.79 us
  transfers between devices with their start and end apart: 10, of which 7 were waited for; matrix products, arithmetic and copies ran while one was open for 4% of the time, Pallas kernels for 0%

profile of v1, /device:TPU:0, one launch (start us, length us, event | category | flops | bytes accessed | tf_op | source)
XLA Modules:
  0.0 105.9 jit_solution(6184102733772753001)
XLA Ops:
  6.5 0.0 all-gather.4.cloned.1.call-start
  6.6 0.7 all-gather.4.cloned.1.call-update
  7.3 0.0 all-gather.6.cloned.1.call-start
  7.3 0.7 all-gather.6.cloned.1.call-update
  8.0 0.0 all-gather.8.cloned.1.call-start
  8.1 3.0 %collective-permute-start = (bf16[1,7168]{1,0:T(2,128)(2,1)S(1)}, bf16[1,7168]{1,0:T(2,128)(2,1)S(1)}, u32[]{:S(2)}, u32[]{:S(2)}) collective-permute-start(bf16[1,7168]{1,0:T(2,128)(2,1)S(1)} %copy-done.1), channel_id=1, source_target_pairs={{0,1},{1,2},{2,3},{3,4},{4,5},{5,6},{6,7},{7,0},{8,9},{9,10},{10,1... | collective-permute-start | bytes 43016 | tf_op jit(solution)/shard_map/ppermute | solution.py:10
  11.1 4.9 %collective-permute-done = bf16[1,7168]{1,0:T(2,128)(2,1)S(1)} collective-permute-done((bf16[1,7168]{1,0:T(2,128)(2,1)S(1)}, bf16[1,7168]{1,0:T(2,128)(2,1)S(1)}, u32[]{:S(2)}, u32[]{:S(2)}) %collective-permute-start) | collective-permute-done | bytes 14368 | tf_op jit(solution)/shard_map/ppermute | solution.py:10
  16.0 0.0 all-gather.8.cloned.1.call-update
  16.0 6.5 %collective-permute-done.1 = bf16[1,7168]{1,0:T(2,128)(2,1)S(1)} collective-permute-done((bf16[1,7168]{1,0:T(2,128)(2,1)S(1)}, bf16[1,7168]{1,0:T(2,128)(2,1)S(1)}, u32[]{:S(2)}, u32[]{:S(2)}) %collective-permute-start.1) | collective-permute-done | bytes 14368 | tf_op jit(solution)/shard_map/ppermute | solution.py:10
  22.6 6.5 %collective-permute-done.2 = bf16[1,7168]{1,0:T(2,128)(2,1)S(1)} collective-permute-done((bf16[1,7168]{1,0:T(2,128)(2,1)S(1)}, bf16[1,7168]{1,0:T(2,128)(2,1)S(1)}, u32[]{:S(2)}, u32[]{:S(2)}) %collective-permute-start.2) | collective-permute-done | bytes 14368 | tf_op jit(solution)/shard_map/ppermute | solution.py:10
  29.1 6.6 %collective-permute-done.3 = bf16[1,7168]{1,0:T(2,128)(2,1)S(1)} collective-permute-done((bf16[1,7168]{1,0:T(2,128)(2,1)S(1)}, bf16[1,7168]{1,0:T(2,128)(2,1)S(1)}, u32[]{:S(2)}, u32[]{:S(2)}) %collective-permute-start.3) | collective-permute-done | bytes 14368 | tf_op jit(solution)/shard_map/ppermute | solution.py:10
  35.7 6.8 %collective-permute-done.4 = bf16[1,7168]{1,0:T(2,128)(2,1)S(1)} collective-permute-done((bf16[1,7168]{1,0:T(2,128)(2,1)S(1)}, bf16[1,7168]{1,0:T(2,128)(2,1)S(1)}, u32[]{:S(2)}, u32[]{:S(2)}) %collective-permute-start.4) | collective-permute-done | bytes 14368 | tf_op jit(solution)/shard_map/ppermute | solution.py:10
  42.5 6.6 %collective-permute-done.5 = bf16[1,7168]{1,0:T(2,128)(2,1)S(1)} collective-permute-done((bf16[1,7168]{1,0:T(2,128)(2,1)S(1)}, bf16[1,7168]{1,0:T(2,128)(2,1)S(1)}, u32[]{:S(2)}, u32[]{:S(2)}) %collective-permute-start.5) | collective-permute-done | bytes 14368 | tf_op jit(solution)/shard_map/ppermute | solution.py:10
  49.1 0.7 dynamic-slice.2
  49.8 5.9 %collective-permute-done.6 = bf16[1,7168]{1,0:T(2,128)(2,1)S(1)} collective-permute-done((bf16[1,7168]{1,0:T(2,128)(2,1)S(1)}, bf16[1,7168]{1,0:T(2,128)(2,1)S(1)}, u32[]{:S(2)}, u32[]{:S(2)}) %collective-permute-start.6) | collective-permute-done | bytes 14368 | tf_op jit(solution)/shard_map/ppermute | solution.py:10
  55.6 0.7 concatenate.6
  56.4 0.6 gather_fusion
  57.0 0.0 all-gather.4.cloned.1.call-done
  57.0 1.9 %fusion.4 = f32[8,128]{1,0:T(8,128)S(1)} fusion(bf16[7168,128]{1,0:T(8,128)(2,1)} %all-gather.4.cloned.1.call-done, bf16[8,7168]{1,0:T(8,128)(2,1)S(1)} %gather_fusion, pred[8]{0:T(512)(128)(4,1)S(1)} %compare_and_fusion), kind=kOutput, calls=%fused_computation.9 | convolution fusion | flops 14737408 | bytes 1953800 | tf_op jit(solution)/shard_map/dot_general | solution.py:28
  58.9 0.0 all-gather.8.cloned.1.call-done
  59.0 2.8 %fusion = f32[8,7168]{1,0:T(8,128)S(1)} fusion(bf16[128,7168]{1,0:T(8,128)(2,1)} %all-gather.8.cloned.1.call-done, bf16[7168,128]{1,0:T(8,128)(2,1)} %all-gather.6.cloned.1.call-done, f32[7168]{0:T(1024)S(1)} %bitcast.13, f32[8]{0:T(128)S(1)} %fusion.11, bf16[8,7168]{1,0:T(8,128)(2,1)S(1)} %gather_fusion, pred[8]{0:T(512)(128)(4,1)S(1)} %compare_and_fusion, ...), kind=kOutput, calls=%fused_computation.3 | convolution fusion | flops 29538304 | bytes 4046888 | tf_op jit(solution)/shard_map/dot_general | solution.py:42
  61.8 0.9 scatter_custom_fusion
  62.7 35.3 %all-reduce.2 = bf16[8,7168]{1,0:T(8,128)(2,1)S(1)} all-reduce(f32[8,7168]{1,0:T(8,128)S(1)} %scatter_custom_fusion), channel_id=2, replica_groups=mesh['groups'=2,'fsdp'=2,'ep'=8] {'ep'}, use_global_device_ids=true, to_apply=%region_1.2.clone | all-reduce | flops 57344 | bytes 344064
  98.0 1.3 %dynamic-slice_convert_fusion = bf16[1,7168]{1,0:T(2,128)(2,1)} fusion(bf16[8,7168]{1,0:T(8,128)(2,1)S(1)} %all-reduce.2, u32[]{:T(128)} %bitcast.5), kind=kLoop, calls=%fused_computation.10 | loop fusion | bytes 28676 | tf_op jit(solution)/shard_map/convert_element_type | solution.py:51
  (23 shorter events, 0.1 us)
Async XLA Ops:
  6.5 42.6 %copy-start = (f32[2,1,8]{2,1,0:T(1,128)S(1)}, f32[2,1,8]{2,1,0:T(1,128)}, u32[]{:S(2)}) copy-start(f32[2,1,8]{2,1,0:T(1,128)} %param.13) | copy-start | bytes 196
  6.5 42.6 %copy-start.4 = (u32[32]{0:T(128)S(1)}, u32[32]{0:T(128)}, u32[]{:S(2)}) copy-start(u32[32]{0:T(128)} %constant.97) | copy-start | bytes 388
  6.5 1.5 %copy-start.1 = (bf16[1,7168]{1,0:T(2,128)(2,1)S(1)}, bf16[1,7168]{1,0:T(2,128)(2,1)}, u32[]{:S(2)}) copy-start(bf16[1,7168]{1,0:T(2,128)(2,1)} %param.7) | copy-start | bytes 43012
  6.5 16.0 %copy-start.2 = (bf16[1,7168]{1,0:T(2,128)(2,1)S(1)}, bf16[1,7168]{1,0:T(2,128)(2,1)}, u32[]{:S(2)}) copy-start(bf16[1,7168]{1,0:T(2,128)(2,1)} %param.11) | copy-start | bytes 43012
  6.5 22.6 %copy-start.3 = (s32[2,1,8]{2,1,0:T(1,128)S(1)}, s32[2,1,8]{2,1,0:T(1,128)}, u32[]{:S(2)}) copy-start(s32[2,1,8]{2,1,0:T(1,128)} %param.12) | copy-start | bytes 196
  6.5 50.5 %all-gather.4.cloned.1.call-start = ((), (), s32[]{:S(2)}) async-start(), calls=%async_computation | async-start | bytes 2752512 | tf_op jit(solution)/shard_map/all_gather | solution.py:30
  7.3 51.7 %all-gather.6.cloned.1.call-start = ((), (), s32[]{:S(2)}) async-start(), calls=%async_computation.1 | async-start | bytes 2752512 | tf_op jit(solution)/shard_map/all_gather | solution.py:35
  8.0 50.9 %all-gather.8.cloned.1.call-start = ((), (), s32[]{:S(2)}) async-start(), calls=%async_computation.2 | async-start | bytes 2752512 | tf_op jit(solution)/shard_map/all_gather | solution.py:44
  8.1 7.9 %collective-permute-start = (bf16[1,7168]{1,0:T(2,128)(2,1)S(1)}, bf16[1,7168]{1,0:T(2,128)(2,1)S(1)}, u32[]{:S(2)}, u32[]{:S(2)}) collective-permute-start(bf16[1,7168]{1,0:T(2,128)(2,1)S(1)} %copy-done.1), channel_id=1, source_target_pairs={{0,1},{1,2},{2,3},{3,4},{4,5},{5,6},{6,7},{7,0},{8,9},{9,10},{10,1... | collective-permute-start | bytes 43016 | tf_op jit(solution)/shard_map/ppermute | solution.py:10
  16.0 6.6 %collective-permute-start.1 = (bf16[1,7168]{1,0:T(2,128)(2,1)S(1)}, bf16[1,7168]{1,0:T(2,128)(2,1)S(1)}, u32[]{:S(2)}, u32[]{:S(2)}) collective-permute-start(bf16[1,7168]{1,0:T(2,128)(2,1)S(1)} %collective-permute-done), channel_id=1, source_target_pairs={{0,1},{1,2},{2,3},{3,4},{4,5},{5,6},{6,7},{7,0},{8,9},{9,10},{10,1... | collective-permute-start | bytes 43016 | tf_op jit(solution)/shard_map/ppermute | solution.py:10
  22.5 6.6 %collective-permute-start.2 = (bf16[1,7168]{1,0:T(2,128)(2,1)S(1)}, bf16[1,7168]{1,0:T(2,128)(2,1)S(1)}, u32[]{:S(2)}, u32[]{:S(2)}) collective-permute-start(bf16[1,7168]{1,0:T(2,128)(2,1)S(1)} %collective-permute-done.1), channel_id=1, source_target_pairs={{0,1},{1,2},{2,3},{3,4},{4,5},{5,6},{6,7},{7,0},{8,9},{9,10},{10,1... | collective-permute-start | bytes 43016 | tf_op jit(solution)/shard_map/ppermute | solution.py:10
  29.1 6.6 %collective-permute-start.3 = (bf16[1,7168]{1,0:T(2,128)(2,1)S(1)}, bf16[1,7168]{1,0:T(2,128)(2,1)S(1)}, u32[]{:S(2)}, u32[]{:S(2)}) collective-permute-start(bf16[1,7168]{1,0:T(2,128)(2,1)S(1)} %collective-permute-done.2), channel_id=1, source_target_pairs={{0,1},{1,2},{2,3},{3,4},{4,5},{5,6},{6,7},{7,0},{8,9},{9,10},{10,1... | collective-permute-start | bytes 43016 | tf_op jit(solution)/shard_map/ppermute | solution.py:10
  35.7 6.8 %collective-permute-start.4 = (bf16[1,7168]{1,0:T(2,128)(2,1)S(1)}, bf16[1,7168]{1,0:T(2,128)(2,1)S(1)}, u32[]{:S(2)}, u32[]{:S(2)}) collective-permute-start(bf16[1,7168]{1,0:T(2,128)(2,1)S(1)} %collective-permute-done.3), channel_id=1, source_target_pairs={{0,1},{1,2},{2,3},{3,4},{4,5},{5,6},{6,7},{7,0},{8,9},{9,10},{10,1... | collective-permute-start | bytes 43016 | tf_op jit(solution)/shard_map/ppermute | solution.py:10
  42.5 6.6 %collective-permute-start.5 = (bf16[1,7168]{1,0:T(2,128)(2,1)S(1)}, bf16[1,7168]{1,0:T(2,128)(2,1)S(1)}, u32[]{:S(2)}, u32[]{:S(2)}) collective-permute-start(bf16[1,7168]{1,0:T(2,128)(2,1)S(1)} %collective-permute-done.4), channel_id=1, source_target_pairs={{0,1},{1,2},{2,3},{3,4},{4,5},{5,6},{6,7},{7,0},{8,9},{9,10},{10,1... | collective-permute-start | bytes 43016 | tf_op jit(solution)/shard_map/ppermute | solution.py:10
  49.1 6.6 %collective-permute-start.6 = (bf16[1,7168]{1,0:T(2,128)(2,1)S(1)}, bf16[1,7168]{1,0:T(2,128)(2,1)S(1)}, u32[]{:S(2)}, u32[]{:S(2)}) collective-permute-start(bf16[1,7168]{1,0:T(2,128)(2,1)S(1)} %collective-permute-done.5), channel_id=1, source_target_pairs={{0,1},{1,2},{2,3},{3,4},{4,5},{5,6},{6,7},{7,0},{8,9},{9,10},{10,1... | collective-permute-start | bytes 43016 | tf_op jit(solution)/shard_map/ppermute | solution.py:10
Sparse Core Ops, SparseCore 0:
  8.9 12.8 all-gather.3
  23.4 11.3 all-gather.5
  36.3 11.3 all-gather.7
